TPU v7x, 32 devices: a whole 2x2x4 slice. The times are simulated.
32 devices in a mesh: group: 4 (over y, x), leaf: 8 (over z, core).
Axes of the slice: x: 2, y: 2, z: 4, core: 2. Of those that a mesh axis runs over, the one named last changes fastest.
Arguments:
- points: bfloat16 [65536, 64], P(('group', 'leaf')), may hold values from -1.1953125 to 1.1953125
- ordering: int32 [32, 2048], P(('group', 'leaf')), may hold values from 0 to 2047, each once within a row
- iterate: float32 [65536, 128], P(('group', 'leaf')), may hold values from -6 to 6
- target: float32 [65536, 128], P(('group', 'leaf')), may hold values from -18 to 18
- step_size: float32 [128], replicated, may hold values from 0.1 to 0.5
- leaf_basis: bfloat16 [65536, 256], P(('group', 'leaf')), may hold values from -0.125 to 0.125
- transfer: bfloat16 [32, 256, 256], P(('group', 'leaf')), may hold values from -0.375 to 0.375
- leaf_skeleton: bfloat16 [32, 256, 64], P(('group', 'leaf')), may hold values from -0.8984375 to 0.8984375
- cluster_skeleton: bfloat16 [4, 256, 64], P('group'), may hold values from -1.1953125 to 1.1953125
- near_table: int32 [32, 8], P(('group', 'leaf')), may hold values from 0 to 1, as said below
- far_table: int32 [32, 8], P(('group', 'leaf')), may hold values from 0 to 1, as said below
- cluster_far: int32 [4, 4], P('group'), may hold values from 0 to 1, as said below
Outputs:
- updated: float32 [65536, 128], P(('group', 'leaf'))
Inputs may be any that keep to these rules, and one draw needn't show every extreme that they name: `near_table`: entries 0 or 1; each leaf's own place is 1; a 1 stands only at places at most 3 away from the leaf's own place; each row has at most 7 ones, and some row exactly 7. `far_table`: entries 0 or 1, never 1 where near_table is 1. `cluster_far`: entries 0 or 1, zero on the diagonal. `ordering`: each row is a permutation.
All inputs are finite; a program needn't handle non-finite values.
Results may differ from a plain program's by a relative error of at most 0.0044.
Values may be sent and summed in bfloat16 or wider, within the bound.
No kernel may reach another device: no remote copies, remote signals or barrier semaphores. Data moves between devices by JAX's collectives and lax.ppermute only.
A program may use at most 128 MiB of HBM per device.

v0:
```python
import jax
import jax.numpy as jnp
from jax import lax
from jax.sharding import PartitionSpec as P

NEAR_MOST = 7


def passed_along(block, axis, distance):
    devices = range(lax.axis_size(axis))
    route = [(i - distance, i) for i in devices if i - distance in devices]
    return lax.ppermute(block, axis, route)


def kernel_tile(left, right):
    left_f = left.astype(jnp.float32)
    right_f = right.astype(jnp.float32)
    left_sq = jnp.sum(left_f * left_f, axis=1)
    right_sq = jnp.sum(right_f * right_f, axis=1)
    inner = lax.dot_general(
        left, right, (((1,), (1,)), ((), ())), preferred_element_type=jnp.float32
    )
    return jnp.exp(-(left_sq[:, None] + right_sq[None, :] - 2.0 * inner)).astype(jnp.bfloat16)


def body(
    points,
    ordering,
    iterate,
    target,
    step_size,
    leaf_basis,
    transfer,
    leaf_skeleton,
    cluster_skeleton,
    near_table,
    far_table,
    cluster_far,
):
    leaf_rows = points.shape[0]
    point_cols = points.shape[1]
    rhs_cols = iterate.shape[1]
    rank_cols = leaf_basis.shape[1]
    rounded = iterate.astype(jnp.bfloat16)
    coeffs = lax.dot_general(
        leaf_basis, rounded, (((0,), (0,)), ((), ())), preferred_element_type=jnp.float32
    ).astype(jnp.bfloat16)
    near_row = near_table[0]
    far_row = far_table[0]
    own_transfer = transfer[0]
    reach = (NEAR_MOST - 1) // 2
    joined = jnp.concatenate([points, rounded], axis=1)
    below_blocks = []
    above_blocks = []
    passing_below = joined
    passing_above = joined
    for distance in range(1, reach + 1):
        passing_below = passed_along(passing_below, "leaf", 1)
        passing_above = passed_along(passing_above, "leaf", -1)
        below_blocks.append(passing_below)
        above_blocks.append(passing_above)
    padded = jnp.concatenate(below_blocks[::-1] + [joined] + above_blocks, axis=0)
    myself = lax.axis_index("leaf")
    cluster_size = near_row.shape[0]

    def window_visit(position, summed):
        place = myself + position - reach
        inside = (place >= 0) & (place < cluster_size)
        listed = lax.dynamic_index_in_dim(
            near_row, jnp.clip(place, 0, cluster_size - 1), 0, keepdims=False
        )
        block = lax.dynamic_slice_in_dim(padded, position * leaf_rows, leaf_rows, 0)
        other_points = block[:, :point_cols]
        other_values = block[:, point_cols:]

        def include(current):
            return current + jnp.dot(
                kernel_tile(points, other_points), other_values, preferred_element_type=jnp.float32
            )

        return lax.cond(inside & (listed > 0), include, lambda current: current, summed)

    near_sum = lax.fori_loop(
        0, 2 * reach + 1, window_visit, jnp.zeros((leaf_rows, rhs_cols), jnp.float32)
    )

    def far_visit(skeletons, values):

        def visit(position, summed):
            listed = lax.dynamic_index_in_dim(far_row, position, 0, keepdims=False)

            def include(current):
                return current + jnp.dot(
                    kernel_tile(leaf_skeleton[0], skeletons[position]),
                    values[position],
                    preferred_element_type=jnp.float32,
                )

            return lax.cond(listed > 0, include, lambda current: current, summed)

        return visit

    empty_far = jnp.zeros((rank_cols, rhs_cols), jnp.float32)
    skeletons = lax.all_gather(leaf_skeleton, "leaf", axis=0, tiled=True)
    values = lax.all_gather(coeffs[None], "leaf", axis=0, tiled=True)
    far_sum = lax.fori_loop(0, skeletons.shape[0], far_visit(skeletons, values), empty_far)
    upward_terms = lax.dot_general(
        own_transfer, coeffs, (((0,), (0,)), ((), ())), preferred_element_type=jnp.float32
    )
    upper = lax.psum(upward_terms, "leaf").astype(jnp.bfloat16)
    cluster_row = cluster_far[0]
    skeletons = lax.all_gather(cluster_skeleton, "group", axis=0, tiled=True)
    values = lax.all_gather(upper[None], "group", axis=0, tiled=True)

    def visit(position, summed):
        listed = lax.dynamic_index_in_dim(cluster_row, position, 0, keepdims=False)

        def include(current):
            return current + jnp.dot(
                kernel_tile(cluster_skeleton[0], skeletons[position]),
                values[position],
                preferred_element_type=jnp.float32,
            )

        return lax.cond(listed > 0, include, lambda current: current, summed)

    lower = lax.fori_loop(0, skeletons.shape[0], visit, empty_far).astype(jnp.bfloat16)
    local = (far_sum + jnp.dot(own_transfer, lower, preferred_element_type=jnp.float32)).astype(
        jnp.bfloat16
    )
    image = jnp.dot(leaf_basis, local, preferred_element_type=jnp.float32) + near_sum
    sorted_target = target[ordering[0]]
    return iterate + step_size[None, :] * (sorted_target - image)


def solution(mesh):
    return jax.shard_map(
        body,
        mesh=mesh,
        in_specs=(
            P(("group", "leaf"), None),
            P(("group", "leaf"), None),
            P(("group", "leaf"), None),
            P(("group", "leaf"), None),
            P(),
            P(("group", "leaf"), None),
            P(("group", "leaf"), None, None),
            P(("group", "leaf"), None, None),
            P("group", None, None),
            P(("group", "leaf"), None),
            P(("group", "leaf"), None),
            P("group", None),
        ),
        out_specs=P(("group", "leaf"), None),
        check_vma=False,
    )
```

profile of v0, /device:TPU:15, one launch (start us, length us, event | category | flops | bytes accessed | tf_op | source)
XLA Modules:
  0.0 278.6 jit_solution(15546868874311557150)
XLA Ops:
  0.0 1.7 copy.46
  2.7 1.9 pad_maximum_fusion
  4.6 3.9 %collective-permute-start = (bf16[2048,192]{0,1:T(8,128)(2,1)}, bf16[2048,192]{0,1:T(8,128)(2,1)}, u32[]{:S(2)}, u32[]{:S(2)}) collective-permute-start(bf16[2048,192]{0,1:T(8,128)(2,1)} %pad_maximum_fusion), channel_id=1, source_target_pairs={{0,1},{1,2},{2,3},{3,4},{4,5},{5,6},{6,7},{8,9},{9,10},{10,11},{11... | collective-permute-start | bytes 2359304 | tf_op jit(solution)/shard_map/ppermute | solution.py:12
  8.5 1.9 collective-permute-start.3
  10.4 7.3 %collective-permute-done = bf16[2048,192]{0,1:T(8,128)(2,1)} collective-permute-done((bf16[2048,192]{0,1:T(8,128)(2,1)}, bf16[2048,192]{0,1:T(8,128)(2,1)}, u32[]{:S(2)}, u32[]{:S(2)}) %collective-permute-start) | collective-permute-done | bytes 786464 | tf_op jit(solution)/shard_map/ppermute | solution.py:12
  17.7 4.4 %collective-permute-start.1 = (bf16[2048,192]{0,1:T(8,128)(2,1)}, bf16[2048,192]{0,1:T(8,128)(2,1)}, u32[]{:S(2)}, u32[]{:S(2)}) collective-permute-start(bf16[2048,192]{0,1:T(8,128)(2,1)} %collective-permute-done), channel_id=1, source_target_pairs={{0,1},{1,2},{2,3},{3,4},{4,5},{5,6},{6,7},{8,9},{9,10},{10,11},{11... | collective-permute-start | bytes 2359304 | tf_op jit(solution)/shard_map/ppermute | solution.py:12
  22.8 25.1 %all-reduce.1 = bf16[256,128]{0,1:T(8,128)(2,1)S(1)} all-reduce(f32[256,128]{0,1:T(8,128)S(1)} %convolution_bitcast_fusion.2), channel_id=1, replica_groups=mesh['group'=4,'leaf'=8] {'leaf'}, use_global_device_ids=true, to_apply=%region_6.7 | all-reduce | flops 32768 | bytes 196608 | tf_op jit(solution)/shard_map/psum | solution.py:110
  47.9 17.8 %all-gather = bf16[2048,128]{1,0:T(8,128)(2,1)} all-gather(bf16[256,128]{1,0:T(8,128)(2,1)S(1)} %convolution_convert_fusion), channel_id=2, replica_groups=mesh['group'=4,'leaf'=8] {'leaf'}, dimensions={0}, use_global_device_ids=true | all-gather | bytes 589824 | tf_op jit(solution)/shard_map/all_gather | solution.py:105
  65.8 2.1 collective-permute-start.4
  67.8 4.1 %collective-permute-start.2 = (bf16[2048,192]{0,1:T(8,128)(2,1)}, bf16[2048,192]{0,1:T(8,128)(2,1)}, u32[]{:S(2)}, u32[]{:S(2)}) collective-permute-start(bf16[2048,192]{0,1:T(8,128)(2,1)} %collective-permute-done.1), channel_id=1, source_target_pairs={{0,1},{1,2},{2,3},{3,4},{4,5},{5,6},{6,7},{8,9},{9,10},{10,11},{11... | collective-permute-start | bytes 2359304 | tf_op jit(solution)/shard_map/ppermute | solution.py:12
  71.9 20.0 %all_gather.12 = bf16[8,256,64]{1,2,0:T(8,128)(2,1)} all-gather(bf16[1,256,64]{1,2,0:T(8,128)(2,1)S(1)} %copy-done.8), channel_id=1, replica_groups=mesh['group'=4,'leaf'=8] {'leaf'}, dimensions={0}, use_global_device_ids=true | all-gather | bytes 294912 | tf_op jit(solution)/shard_map/all_gather | solution.py:104
  93.1 1.9 copy.37
  95.7 17.8 %while.50 = (s32[]{:T(128)}, f32[256,128]{1,0:T(8,128)}, s32[8]{0:T(128)}, bf16[1,256,64]{2,1,0:T(8,128)(2,1)S(1)}, bf16[8,256,64]{2,1,0:T(8,128)(2,1)}, /*index...) while((s32[]{:T(128)}, f32[256,128]{1,0:T(8,128)}, s32[8]{0:T(128)}, bf16[1,256,64]{2,1,0:T(8,128)(2,1)S(1)}, ...), condition=%wide.region_5.6_spmd, body=%wide.region_0.5_spmd.sunk | while | flops 25624072 | bytes 496837 | solution.py:106
  99.4 1.2 dynamic_slice.77
  101.2 1.2 dynamic_slice.77
  103.1 1.2 dynamic_slice.77
  104.9 1.2 dynamic_slice.77
  106.8 1.2 dynamic_slice.77
  110.4 3.1 %conditional.6 = (f32[256,128]{1,0:T(8,128)}) conditional(s32[]{:T(128)} %bitcast.109, f32[256,128]{1,0:T(8,128)} %get-tuple-element.740, (bf16[1,256,64]{2,1,0:T(8,128)(2,1)S(1)}, s32[]{:T(128)}, bf16[8,256,64]{2,1,0:T(8,128)(2,1)}, bf16[8,256,128]{2,1,0:T(8,128)(2,1)}, f32[256,128]{1,0:T(8,128)}) %tuple.135), branch_computations={%region_1.1_spmd, %region_2.4_spmd} | conditional | flops 25624068 | bytes 496686 | solution.py:99
  111.4 2.1 fusion.6
  113.5 1.7 copy.41
  115.2 13.8 %all-gather.1 = bf16[1024,128]{0,1:T(8,128)(2,1)} all-gather(bf16[256,128]{0,1:T(8,128)(2,1)S(1)} %all-reduce.1), channel_id=3, replica_groups=mesh['group'=4,'leaf'=8] {'group'}, dimensions={0}, use_global_device_ids=true | all-gather | bytes 327680 | tf_op jit(solution)/shard_map/all_gather | solution.py:113
  128.9 1.8 copy.48
  131.6 7.2 %all_gather.14 = bf16[4,256,64]{1,2,0:T(8,128)(2,1)} all-gather(bf16[1,256,64]{1,2,0:T(8,128)(2,1)} %param.32), channel_id=1, replica_groups=mesh['group'=4,'leaf'=8] {'group'}, dimensions={0}, use_global_device_ids=true | all-gather | bytes 163840 | tf_op jit(solution)/shard_map/all_gather | solution.py:112
  138.8 1.8 copy.39
  140.6 7.6 %gather_fusion = f32[2048,128]{1,0:T(8,128)} fusion(f32[2048,128]{1,0:T(8,128)S(1)} %copy-done.1, s32[2048]{0:T(1024)S(1)} %broadcast_clamp_fusion), kind=kCustom, calls=%fused_computation | custom fusion | bytes 2105344 | tf_op jit(solution)/shard_map/gather | solution.py:132
  148.2 2.6 copy.45
  150.8 9.8 %while.51 = (s32[]{:T(128)}, f32[256,128]{1,0:T(8,128)S(1)}, s32[4]{0:T(128)S(1)}, bf16[1,256,64]{2,1,0:T(8,128)(2,1)S(1)}, bf16[4,256,64]{2,1,0:T(8,128)(2,1)},...) while((s32[]{:T(128)}, f32[256,128]{1,0:T(8,128)S(1)}, s32[4]{0:T(128)S(1)}, ...), condition=%wide.region_12.13_spmd, body=%wide.region_7.12_spmd.sunk | while | flops 25624072 | bytes 496837 | solution.py:127
  153.4 2.3 conditional.7
  154.4 1.3 fusion.28
  157.0 2.3 conditional.7
  158.0 1.3 fusion.28
  160.7 9.4 %collective-permute-start.5 = (bf16[2048,192]{0,1:T(8,128)(2,1)}, bf16[2048,192]{0,1:T(8,128)(2,1)S(1)}, u32[]{:S(2)}, u32[]{:S(2)}) collective-permute-start(bf16[2048,192]{0,1:T(8,128)(2,1)} %collective-permute-done.4), channel_id=1, source_target_pairs={{1,0},{2,1},{3,2},{4,3},{5,4},{6,5},{7,6},{9,8},{10,9},{11,10},{12... | collective-permute-start | bytes 2359304 | tf_op jit(solution)/shard_map/ppermute | solution.py:12
  170.1 2.2 constant_dynamic-update-slice_fusion.6
  172.3 2.1 constant_dynamic-update-slice_fusion.5
  174.4 2.2 constant_dynamic-update-slice_fusion.4
  177.5 2.2 constant_dynamic-update-slice_fusion.2
  179.7 2.2 constant_dynamic-update-slice_fusion.1
  182.8 9.2 %copy.43 = bf16[14336,192]{1,0:T(8,128)(2,1)} copy(bf16[14336,192]{0,1:T(8,128)(2,1)} %constant_dynamic-update-slice_fusion) | data formatting | bytes 11010048 | tf_op jit(solution)/shard_map/while | solution.py:83
  193.2 77.1 %while.52 = (s32[]{:T(128)}, f32[2048,128]{1,0:T(8,128)}, s32[]{:T(128)}, s32[8]{0:T(128)S(1)}, bf16[2048,64]{1,0:T(8,128)(2,1)S(1)}, /*index=5*/bf16[14336,192]...) while((s32[]{:T(128)}, f32[2048,128]{1,0:T(8,128)}, ...), condition=%wide.region_18.19_spmd, body=%wide.region_13.18_spmd.sunk | while | flops 1632628736 | bytes 3966781 | solution.py:83
  194.5 9.7 %conditional.8 = (f32[2048,128]{1,0:T(8,128)}) conditional(s32[]{:T(128)} %convert_element_type.116, f32[2048,128]{1,0:T(8,128)} %get-tuple-element.708, (bf16[2048,64]{1,0:T(8,128)(2,1)S(1)}, s32[]{:T(128)}, bf16[14336,192]{1,0:T(8,128)(2,1)}, f32[2048,128]{1,0:T(8,128)}) %tuple.139), branch_computations={%region_14.14_spmd, %region_15.17_spmd} | conditional | flops 1632628736 | bytes 3966534 | solution.py:81
  194.5 1.7 multiply_reduce_fusion.4
  196.2 8.0 %convolution_add_fusion = f32[2048,128]{1,0:T(8,128)} fusion(f32[2048,128]{1,0:T(8,128)} %get-tuple-element.471, bf16[2048,64]{1,0:T(8,128)(2,1)S(1)} %get-tuple-element.472, f32[2048]{0:T(1024)S(1)} %get-tuple-element.582, f32[2048]{0:T(1024)S(1)} %get-tuple-element.583, bf16[14336,192]{1,0:T(8,128)(2,1)} %get-tuple-element.473, s32[]{:T(128)S(6)} %select_n.45, ...), kind=kOutput, calls=%fused_computation.47 | convolution fusion | flops 1631846400 | bytes 3425792 | tf_op jit(solution)/shard_map/while/body/eval_jaxpr/cond/branch_1_fun/dot_general | solution.py:77
  205.5 9.7 %conditional.8 = (f32[2048,128]{1,0:T(8,128)}) conditional(s32[]{:T(128)} %convert_element_type.116, f32[2048,128]{1,0:T(8,128)} %get-tuple-element.708, (bf16[2048,64]{1,0:T(8,128)(2,1)S(1)}, s32[]{:T(128)}, bf16[14336,192]{1,0:T(8,128)(2,1)}, f32[2048,128]{1,0:T(8,128)}) %tuple.139), branch_computations={%region_14.14_spmd, %region_15.17_spmd} | conditional | flops 1632628736 | bytes 3966534 | solution.py:81
  205.5 1.7 multiply_reduce_fusion.4
  207.2 8.0 %convolution_add_fusion = f32[2048,128]{1,0:T(8,128)} fusion(f32[2048,128]{1,0:T(8,128)} %get-tuple-element.471, bf16[2048,64]{1,0:T(8,128)(2,1)S(1)} %get-tuple-element.472, f32[2048]{0:T(1024)S(1)} %get-tuple-element.582, f32[2048]{0:T(1024)S(1)} %get-tuple-element.583, bf16[14336,192]{1,0:T(8,128)(2,1)} %get-tuple-element.473, s32[]{:T(128)S(6)} %select_n.45, ...), kind=kOutput, calls=%fused_computation.47 | convolution fusion | flops 1631846400 | bytes 3425792 | tf_op jit(solution)/shard_map/while/body/eval_jaxpr/cond/branch_1_fun/dot_general | solution.py:77
  216.5 9.7 %conditional.8 = (f32[2048,128]{1,0:T(8,128)}) conditional(s32[]{:T(128)} %convert_element_type.116, f32[2048,128]{1,0:T(8,128)} %get-tuple-element.708, (bf16[2048,64]{1,0:T(8,128)(2,1)S(1)}, s32[]{:T(128)}, bf16[14336,192]{1,0:T(8,128)(2,1)}, f32[2048,128]{1,0:T(8,128)}) %tuple.139), branch_computations={%region_14.14_spmd, %region_15.17_spmd} | conditional | flops 1632628736 | bytes 3966534 | solution.py:81
  216.5 1.7 multiply_reduce_fusion.4
  218.2 8.0 %convolution_add_fusion = f32[2048,128]{1,0:T(8,128)} fusion(f32[2048,128]{1,0:T(8,128)} %get-tuple-element.471, bf16[2048,64]{1,0:T(8,128)(2,1)S(1)} %get-tuple-element.472, f32[2048]{0:T(1024)S(1)} %get-tuple-element.582, f32[2048]{0:T(1024)S(1)} %get-tuple-element.583, bf16[14336,192]{1,0:T(8,128)(2,1)} %get-tuple-element.473, s32[]{:T(128)S(6)} %select_n.45, ...), kind=kOutput, calls=%fused_computation.47 | convolution fusion | flops 1631846400 | bytes 3425792 | tf_op jit(solution)/shard_map/while/body/eval_jaxpr/cond/branch_1_fun/dot_general | solution.py:77
  227.5 9.7 %conditional.8 = (f32[2048,128]{1,0:T(8,128)}) conditional(s32[]{:T(128)} %convert_element_type.116, f32[2048,128]{1,0:T(8,128)} %get-tuple-element.708, (bf16[2048,64]{1,0:T(8,128)(2,1)S(1)}, s32[]{:T(128)}, bf16[14336,192]{1,0:T(8,128)(2,1)}, f32[2048,128]{1,0:T(8,128)}) %tuple.139), branch_computations={%region_14.14_spmd, %region_15.17_spmd} | conditional | flops 1632628736 | bytes 3966534 | solution.py:81
  227.5 1.7 multiply_reduce_fusion.4
  229.2 8.0 %convolution_add_fusion = f32[2048,128]{1,0:T(8,128)} fusion(f32[2048,128]{1,0:T(8,128)} %get-tuple-element.471, bf16[2048,64]{1,0:T(8,128)(2,1)S(1)} %get-tuple-element.472, f32[2048]{0:T(1024)S(1)} %get-tuple-element.582, f32[2048]{0:T(1024)S(1)} %get-tuple-element.583, bf16[14336,192]{1,0:T(8,128)(2,1)} %get-tuple-element.473, s32[]{:T(128)S(6)} %select_n.45, ...), kind=kOutput, calls=%fused_computation.47 | convolution fusion | flops 1631846400 | bytes 3425792 | tf_op jit(solution)/shard_map/while/body/eval_jaxpr/cond/branch_1_fun/dot_general | solution.py:77
  238.5 9.7 %conditional.8 = (f32[2048,128]{1,0:T(8,128)}) conditional(s32[]{:T(128)} %convert_element_type.116, f32[2048,128]{1,0:T(8,128)} %get-tuple-element.708, (bf16[2048,64]{1,0:T(8,128)(2,1)S(1)}, s32[]{:T(128)}, bf16[14336,192]{1,0:T(8,128)(2,1)}, f32[2048,128]{1,0:T(8,128)}) %tuple.139), branch_computations={%region_14.14_spmd, %region_15.17_spmd} | conditional | flops 1632628736 | bytes 3966534 | solution.py:81
  238.5 1.7 multiply_reduce_fusion.4
  240.2 8.0 %convolution_add_fusion = f32[2048,128]{1,0:T(8,128)} fusion(f32[2048,128]{1,0:T(8,128)} %get-tuple-element.471, bf16[2048,64]{1,0:T(8,128)(2,1)S(1)} %get-tuple-element.472, f32[2048]{0:T(1024)S(1)} %get-tuple-element.582, f32[2048]{0:T(1024)S(1)} %get-tuple-element.583, bf16[14336,192]{1,0:T(8,128)(2,1)} %get-tuple-element.473, s32[]{:T(128)S(6)} %select_n.45, ...), kind=kOutput, calls=%fused_computation.47 | convolution fusion | flops 1631846400 | bytes 3425792 | tf_op jit(solution)/shard_map/while/body/eval_jaxpr/cond/branch_1_fun/dot_general | solution.py:77
  249.5 9.7 %conditional.8 = (f32[2048,128]{1,0:T(8,128)}) conditional(s32[]{:T(128)} %convert_element_type.116, f32[2048,128]{1,0:T(8,128)} %get-tuple-element.708, (bf16[2048,64]{1,0:T(8,128)(2,1)S(1)}, s32[]{:T(128)}, bf16[14336,192]{1,0:T(8,128)(2,1)}, f32[2048,128]{1,0:T(8,128)}) %tuple.139), branch_computations={%region_14.14_spmd, %region_15.17_spmd} | conditional | flops 1632628736 | bytes 3966534 | solution.py:81
  249.5 1.7 multiply_reduce_fusion.4
  251.2 8.1 %convolution_add_fusion = f32[2048,128]{1,0:T(8,128)} fusion(f32[2048,128]{1,0:T(8,128)} %get-tuple-element.471, bf16[2048,64]{1,0:T(8,128)(2,1)S(1)} %get-tuple-element.472, f32[2048]{0:T(1024)S(1)} %get-tuple-element.582, f32[2048]{0:T(1024)S(1)} %get-tuple-element.583, bf16[14336,192]{1,0:T(8,128)(2,1)} %get-tuple-element.473, s32[]{:T(128)S(6)} %select_n.45, ...), kind=kOutput, calls=%fused_computation.47 | convolution fusion | flops 1631846400 | bytes 3425792 | tf_op jit(solution)/shard_map/while/body/eval_jaxpr/cond/branch_1_fun/dot_general | solution.py:77
  260.5 9.8 %conditional.8 = (f32[2048,128]{1,0:T(8,128)}) conditional(s32[]{:T(128)} %convert_element_type.116, f32[2048,128]{1,0:T(8,128)} %get-tuple-element.708, (bf16[2048,64]{1,0:T(8,128)(2,1)S(1)}, s32[]{:T(128)}, bf16[14336,192]{1,0:T(8,128)(2,1)}, f32[2048,128]{1,0:T(8,128)}) %tuple.139), branch_computations={%region_14.14_spmd, %region_15.17_spmd} | conditional | flops 1632628736 | bytes 3966534 | solution.py:81
  260.5 1.7 multiply_reduce_fusion.4
  262.2 8.1 %convolution_add_fusion = f32[2048,128]{1,0:T(8,128)} fusion(f32[2048,128]{1,0:T(8,128)} %get-tuple-element.471, bf16[2048,64]{1,0:T(8,128)(2,1)S(1)} %get-tuple-element.472, f32[2048]{0:T(1024)S(1)} %get-tuple-element.582, f32[2048]{0:T(1024)S(1)} %get-tuple-element.583, bf16[14336,192]{1,0:T(8,128)(2,1)} %get-tuple-element.473, s32[]{:T(128)S(6)} %select_n.45, ...), kind=kOutput, calls=%fused_computation.47 | convolution fusion | flops 1631846400 | bytes 3425792 | tf_op jit(solution)/shard_map/while/body/eval_jaxpr/cond/branch_1_fun/dot_general | solution.py:77
  270.3 2.5 copy.44
  272.9 3.2 %fusion.56 = f32[2048,128]{0,1:T(8,128)} fusion(f32[2048,128]{0,1:T(8,128)S(1)} %copy-done.3, f32[2048,128]{0,1:T(8,128)} %copy.45, f32[2048,128]{0,1:T(8,128)} %copy.44, bf16[2048,256]{1,0:T(8,128)(2,1)S(1)} %copy-done, f32[256,128]{0,1:T(8,128)S(1)} %copy-done.7, f32[128]{0:T(128)S(1)} %copy-done.10, bf16[1,256,256]{2,1,0:T(8,128)(2,1)S(1)} %copy-done.6, ...), kind=kOutput, calls=%fused_computation.58 | convolution fusion | flops 152141824 | bytes 5636608 | tf_op jit(solution)/shard_map/dot_general | solution.py:131
  276.1 2.5 copy.47
  (70 shorter events, 21.1 us)
Async XLA Ops:
  0.0 22.1 %copy-start = (bf16[2048,256]{1,0:T(8,128)(2,1)S(1)}, bf16[2048,256]{1,0:T(8,128)(2,1)}, u32[]{:S(2)}) copy-start(bf16[2048,256]{1,0:T(8,128)(2,1)} %param.29) | copy-start | bytes 3145732
  0.0 91.9 %copy-start.4 = (bf16[2048,64]{0,1:T(8,128)(2,1)S(1)}, bf16[2048,64]{0,1:T(8,128)(2,1)}, u32[]{:S(2)}) copy-start(bf16[2048,64]{0,1:T(8,128)(2,1)} %param.24) | copy-start | bytes 786436
  0.0 22.6 %copy-start.5 = (bf16[1,256,256]{2,1,0:T(8,128)(2,1)S(1)}, bf16[1,256,256]{2,1,0:T(8,128)(2,1)}, u32[]{:S(2)}) copy-start(bf16[1,256,256]{2,1,0:T(8,128)(2,1)} %param.30) | copy-start | bytes 393220
  0.0 71.9 %copy-start.8 = (bf16[1,256,64]{1,2,0:T(8,128)(2,1)S(1)}, bf16[1,256,64]{1,2,0:T(8,128)(2,1)}, u32[]{:S(2)}) copy-start(bf16[1,256,64]{1,2,0:T(8,128)(2,1)} %param.31) | copy-start | bytes 98308
  1.7 1.0 copy-start.2
  2.7 137.9 %copy-start.9 = (s32[1,2048]{1,0:T(1,128)S(1)}, s32[1,2048]{1,0:T(1,128)}, u32[]{:S(2)}) copy-start(s32[1,2048]{1,0:T(1,128)} %param.25) | copy-start | bytes 24580
  4.6 136.0 %copy-start.1 = (f32[2048,128]{1,0:T(8,128)S(1)}, f32[2048,128]{1,0:T(8,128)}, u32[]{:S(2)}) copy-start(f32[2048,128]{1,0:T(8,128)} %param.27) | copy-start | bytes 3145732
  4.6 13.1 %collective-permute-start = (bf16[2048,192]{0,1:T(8,128)(2,1)}, bf16[2048,192]{0,1:T(8,128)(2,1)}, u32[]{:S(2)}, u32[]{:S(2)}) collective-permute-start(bf16[2048,192]{0,1:T(8,128)(2,1)} %pad_maximum_fusion), channel_id=1, source_target_pairs={{0,1},{1,2},{2,3},{3,4},{4,5},{5,6},{6,7},{8,9},{9,10},{10,11},{11... | collective-permute-start | bytes 2359304 | tf_op jit(solution)/shard_map/ppermute | solution.py:12
  8.5 57.3 %collective-permute-start.3 = (bf16[2048,192]{0,1:T(8,128)(2,1)}, bf16[2048,192]{0,1:T(8,128)(2,1)}, u32[]{:S(2)}, u32[]{:S(2)}) collective-permute-start(bf16[2048,192]{0,1:T(8,128)(2,1)} %pad_maximum_fusion), channel_id=1, source_target_pairs={{1,0},{2,1},{3,2},{4,3},{5,4},{6,5},{7,6},{9,8},{10,9},{11,10},{12... | collective-permute-start | bytes 2359304 | tf_op jit(solution)/shard_map/ppermute | solution.py:12
  17.7 50.1 %collective-permute-start.1 = (bf16[2048,192]{0,1:T(8,128)(2,1)}, bf16[2048,192]{0,1:T(8,128)(2,1)}, u32[]{:S(2)}, u32[]{:S(2)}) collective-permute-start(bf16[2048,192]{0,1:T(8,128)(2,1)} %collective-permute-done), channel_id=1, source_target_pairs={{0,1},{1,2},{2,3},{3,4},{4,5},{5,6},{6,7},{8,9},{9,10},{10,11},{11... | collective-permute-start | bytes 2359304 | tf_op jit(solution)/shard_map/ppermute | solution.py:12
  65.8 94.9 %collective-permute-start.4 = (bf16[2048,192]{0,1:T(8,128)(2,1)}, bf16[2048,192]{0,1:T(8,128)(2,1)}, u32[]{:S(2)}, u32[]{:S(2)}) collective-permute-start(bf16[2048,192]{0,1:T(8,128)(2,1)} %collective-permute-done.3), channel_id=1, source_target_pairs={{1,0},{2,1},{3,2},{4,3},{5,4},{6,5},{7,6},{9,8},{10,9},{11,10},{12... | collective-permute-start | bytes 2359304 | tf_op jit(solution)/shard_map/ppermute | solution.py:12
  67.8 102.2 %collective-permute-start.2 = (bf16[2048,192]{0,1:T(8,128)(2,1)}, bf16[2048,192]{0,1:T(8,128)(2,1)}, u32[]{:S(2)}, u32[]{:S(2)}) collective-permute-start(bf16[2048,192]{0,1:T(8,128)(2,1)} %collective-permute-done.1), channel_id=1, source_target_pairs={{0,1},{1,2},{2,3},{3,4},{4,5},{5,6},{6,7},{8,9},{9,10},{10,11},{11... | collective-permute-start | bytes 2359304 | tf_op jit(solution)/shard_map/ppermute | solution.py:12
  140.6 10.2 %copy-start.11 = (s32[1,4]{1,0:T(1,128)S(1)}, s32[1,4]{1,0:T(1,128)}, u32[]{:S(2)}) copy-start(s32[1,4]{1,0:T(1,128)} %param.35) | copy-start | bytes 52
  160.7 21.2 %collective-permute-start.5 = (bf16[2048,192]{0,1:T(8,128)(2,1)}, bf16[2048,192]{0,1:T(8,128)(2,1)S(1)}, u32[]{:S(2)}, u32[]{:S(2)}) collective-permute-start(bf16[2048,192]{0,1:T(8,128)(2,1)} %collective-permute-done.4), channel_id=1, source_target_pairs={{1,0},{2,1},{3,2},{4,3},{5,4},{6,5},{7,6},{9,8},{10,9},{11,10},{12... | collective-permute-start | bytes 2359304 | tf_op jit(solution)/shard_map/ppermute | solution.py:12
  182.8 10.3 %copy-start.12 = (s32[1,8]{1,0:T(1,128)S(1)}, s32[1,8]{1,0:T(1,128)}, u32[]{:S(2)}) copy-start(s32[1,8]{1,0:T(1,128)} %param.33) | copy-start | bytes 100
  193.1 79.7 %copy-start.3 = (f32[2048,128]{0,1:T(8,128)S(1)}, f32[2048,128]{0,1:T(8,128)}, u32[]{:S(2)}) copy-start(f32[2048,128]{0,1:T(8,128)} %copy-done.2) | copy-start | bytes 3145732
  193.1 79.7 %copy-start.6 = (bf16[1,256,256]{2,1,0:T(8,128)(2,1)S(1)}, bf16[1,256,256]{2,1,0:T(8,128)(2,1)}, u32[]{:S(2)}) copy-start(bf16[1,256,256]{2,1,0:T(8,128)(2,1)} %param.30) | copy-start | bytes 393220
  193.1 79.7 %copy-start.7 = (f32[256,128]{0,1:T(8,128)S(1)}, f32[256,128]{0,1:T(8,128)}, u32[]{:S(2)}) copy-start(f32[256,128]{0,1:T(8,128)} %copy.41) | copy-start | bytes 393220
  193.2 79.7 %copy-start.10 = (f32[128]{0:T(128)S(1)}, f32[128]{0:T(128)}, u32[]{:S(2)}) copy-start(f32[128]{0:T(128)} %param.28) | copy-start | bytes 1540
where the time goes:
time: 281 us; the launch traced here: 279 us
  blocking collectives  84 us (30%)
  local copies, waits for them, and re-layouts  66.5 us (24%)
  matrix products  65 us (23%)
  starting transfers between devices  25.7 us (9%)
  other arithmetic  17.5 us (6%)
  loops' own time  12.3 us (4%)
  waiting for transfers between devices  7.31 us (3%)
    dot_general x7, matrix products, include(): jnp.dot(kernel_tile(points, other_points), other_values, preferred_elemen...  56.4 us
    ppermute x6, starting transfers between devices, passed_along(): return lax.ppermute(block, axis, route)  25.7 us
    psum x1, blocking collectives, body(): upper = lax.psum(upward_terms, 'leaf').astype(jnp.bfloat16)  25.1 us
    all_gather x1, blocking collectives, body(): skeletons = lax.all_gather(leaf_skeleton, 'leaf', axis=0, tiled=True)  20 us
    all_gather x1, blocking collectives, body(): values = lax.all_gather(coeffs[None], 'leaf', axis=0, tiled=True)  17.8 us
    reduce_sum x10, other arithmetic, kernel_tile(): right_sq = jnp.sum(right_f * right_f, axis=1)  14.6 us
    all_gather x1, blocking collectives, body(): values = lax.all_gather(upper[None], 'group', axis=0, tiled=True)  13.8 us
    unnamed x32, local copies, waits for them, and re-layouts  13.4 us
  transfers between devices with their start and end apart: 6, of which 1 were waited for; matrix products, arithmetic and copies ran while one was open for 19% of the time, Pallas kernels for 0%

commit v1 on v0

--- a/solution.py
+++ b/solution.py
@@ -110,7 +110,15 @@
     upper = lax.psum(upward_terms, "leaf").astype(jnp.bfloat16)
     cluster_row = cluster_far[0]
     skeletons = lax.all_gather(cluster_skeleton, "group", axis=0, tiled=True)
-    values = lax.all_gather(upper[None], "group", axis=0, tiled=True)
+    block_2 = upper[None]
+    size = lax.axis_size("group")
+    forward = [(i_2, (i_2 + 1) % size) for i_2 in range(size)]
+    parts = [block_2]
+    for far in range(1, size):
+        parts = [lax.ppermute(parts[0], "group", forward), *parts]
+    out = jnp.concatenate(parts, axis=0)
+    offset = (lax.axis_index("group") + 1) * parts[-1].shape[0]
+    values = jnp.roll(out, offset, axis=0)
 
     def visit(position, summed):
         listed = lax.dynamic_index_in_dim(cluster_row, position, 0, keepdims=False)

time: 281 us -> 270 us (0.961)
  blocking collectives: 84 us -> 71.5 us
  waiting for transfers between devices: 7.31 us -> 2.13 us
  starting transfers between devices: 25.7 us -> 30.7 us
    all_gather x1 -> x0, blocking collectives: 13.8 us -> none  [body(): values = lax.all_gather(upper[None], 'group', axis=0, tiled=True)]
    ppermute x6, waiting for transfers between devices: 7.31 us -> 0.12 us  [passed_along(): return lax.ppermute(block, axis, route)]
    unnamed x32 -> x49, local copies, waits for them, and re-layouts: 13.4 us -> 17.3 us
    ppermute x0 -> x3, starting transfers between devices: none -> 3.57 us  [body(): parts = [lax.ppermute(parts[0], 'group', forward), *parts]]
    all_gather x1, blocking collectives: 20 us -> 17 us  [body(): skeletons = lax.all_gather(leaf_skeleton, 'leaf', axis=0, tiled=True)]
  transfers between devices with their start and end apart: 6 -> 9, of which waited for: 1 -> 2; matrix products, arithmetic and copies ran while one was open for 19% -> 21% of each run, Pallas kernels for 0% -> 0%
where the time goes in v1:
time: 270 us; the launch traced here: 267 us
  blocking collectives  71.5 us (26%)
  local copies, waits for them, and re-layouts  68.2 us (25%)
  matrix products  64.7 us (24%)
  starting transfers between devices  30.7 us (11%)
  other arithmetic  17.7 us (7%)
  loops' own time  12 us (4%)
    dot_general x7, matrix products, include(): jnp.dot(kernel_tile(points, other_points), other_values, preferred_elemen...  56.4 us
    ppermute x6, starting transfers between devices, passed_along(): return lax.ppermute(block, axis, route)  27.1 us
    psum x1, blocking collectives, body(): upper = lax.psum(upward_terms, 'leaf').astype(jnp.bfloat16)  26.7 us
    all_gather x1, blocking collectives, body(): values = lax.all_gather(coeffs[None], 'leaf', axis=0, tiled=True)  20.6 us
    unnamed x49, local copies, waits for them, and re-layouts  17.3 us
    all_gather x1, blocking collectives, body(): skeletons = lax.all_gather(leaf_skeleton, 'leaf', axis=0, tiled=True)  17 us
    reduce_sum x10, other arithmetic, kernel_tile(): right_sq = jnp.sum(right_f * right_f, axis=1)  14.6 us
    while x3, local copies, waits for them, and re-layouts, body(): lax.fori_loop(0, 2 * reach + 1, window_visit, jnp.zeros((leaf_rows, rhs_c...  11.1 us
  transfers between devices with their start and end apart: 9, of which 2 were waited for; matrix products, arithmetic and copies ran while one was open for 21% of the time, Pallas kernels for 0%

profile of v1, /device:TPU:15, one launch (start us, length us, event | category | flops | bytes accessed | tf_op | source)
XLA Modules:
  0.0 267.4 jit_solution(8949136111322257390)
XLA Ops:
  0.0 1.7 copy.46
  2.8 2.0 pad_maximum_fusion
  4.8 3.8 %collective-permute-start.3 = (bf16[2048,192]{0,1:T(8,128)(2,1)}, bf16[2048,192]{0,1:T(8,128)(2,1)}, u32[]{:S(2)}, u32[]{:S(2)}) collective-permute-start(bf16[2048,192]{0,1:T(8,128)(2,1)} %pad_maximum_fusion), channel_id=1, source_target_pairs={{0,1},{1,2},{2,3},{3,4},{4,5},{5,6},{6,7},{8,9},{9,10},{10,11},{11... | collective-permute-start | bytes 2359304 | tf_op jit(solution)/shard_map/ppermute | solution.py:12
  8.5 1.9 collective-permute-start.6
  11.1 26.7 %all-reduce.1 = bf16[256,128]{0,1:T(8,128)(2,1)S(1)} all-reduce(f32[256,128]{0,1:T(8,128)S(1)} %convolution_bitcast_fusion.2), channel_id=1, replica_groups=mesh['group'=4,'leaf'=8] {'leaf'}, use_global_device_ids=true, to_apply=%region_6.7 | all-reduce | flops 32768 | bytes 196608 | tf_op jit(solution)/shard_map/psum | solution.py:110
  38.2 3.8 %collective-permute-start.4 = (bf16[2048,192]{0,1:T(8,128)(2,1)}, bf16[2048,192]{0,1:T(8,128)(2,1)}, u32[]{:S(2)}, u32[]{:S(2)}) collective-permute-start(bf16[2048,192]{0,1:T(8,128)(2,1)} %collective-permute-done.3), channel_id=1, source_target_pairs={{0,1},{1,2},{2,3},{3,4},{4,5},{5,6},{6,7},{8,9},{9,10},{10,11},{11... | collective-permute-start | bytes 2359304 | tf_op jit(solution)/shard_map/ppermute | solution.py:12
  42.0 20.6 %all-gather = bf16[2048,128]{1,0:T(8,128)(2,1)} all-gather(bf16[256,128]{1,0:T(8,128)(2,1)S(1)} %convolution_convert_fusion), channel_id=2, replica_groups=mesh['group'=4,'leaf'=8] {'leaf'}, dimensions={0}, use_global_device_ids=true | all-gather | bytes 589824 | tf_op jit(solution)/shard_map/all_gather | solution.py:105
  63.8 2.0 collective-permute-done.1
  65.8 2.1 collective-permute-start.2
  67.9 17.0 %all_gather.9 = bf16[8,256,64]{1,2,0:T(8,128)(2,1)} all-gather(bf16[1,256,64]{1,2,0:T(8,128)(2,1)S(1)} %copy-done.13), channel_id=1, replica_groups=mesh['group'=4,'leaf'=8] {'leaf'}, dimensions={0}, use_global_device_ids=true | all-gather | bytes 294912 | tf_op jit(solution)/shard_map/all_gather | solution.py:104
  86.9 7.2 %all_gather.11 = bf16[4,256,64]{1,2,0:T(8,128)(2,1)} all-gather(bf16[1,256,64]{1,2,0:T(8,128)(2,1)} %param.32), channel_id=1, replica_groups=mesh['group'=4,'leaf'=8] {'group'}, dimensions={0}, use_global_device_ids=true | all-gather | bytes 163840 | tf_op jit(solution)/shard_map/all_gather | solution.py:112
  94.1 1.8 copy.39
  95.9 2.0 copy.37
  98.5 18.6 %while.50 = (s32[]{:T(128)}, f32[256,128]{1,0:T(8,128)}, s32[8]{0:T(128)}, bf16[1,256,64]{2,1,0:T(8,128)(2,1)S(1)}, bf16[8,256,64]{2,1,0:T(8,128)(2,1)}, /*index...) while((s32[]{:T(128)}, f32[256,128]{1,0:T(8,128)}, s32[8]{0:T(128)}, bf16[1,256,64]{2,1,0:T(8,128)(2,1)S(1)}, ...), condition=%wide.region_5.6_spmd, body=%wide.region_0.5_spmd.sunk | while | flops 25624072 | bytes 496837 | solution.py:106
  100.5 1.3 dynamic_slice.83
  102.4 1.3 dynamic_slice.83
  104.3 1.3 dynamic_slice.83
  106.3 1.3 dynamic_slice.83
  108.2 1.3 dynamic_slice.83
  110.2 1.3 dynamic_slice.83
  112.1 1.3 dynamic_slice.83
  114.0 3.1 %conditional.6 = (f32[256,128]{1,0:T(8,128)}) conditional(s32[]{:T(128)} %bitcast.113, f32[256,128]{1,0:T(8,128)} %get-tuple-element.740, (bf16[1,256,64]{2,1,0:T(8,128)(2,1)S(1)}, s32[]{:T(128)}, bf16[8,256,64]{2,1,0:T(8,128)(2,1)}, bf16[8,256,128]{2,1,0:T(8,128)(2,1)}, f32[256,128]{1,0:T(8,128)}) %tuple.135), branch_computations={%region_1.1_spmd, %region_2.4_spmd} | conditional | flops 25624068 | bytes 496686 | solution.py:99
  115.0 2.1 fusion.6
  117.1 1.7 copy.41
  118.8 7.6 %gather_fusion = f32[2048,128]{1,0:T(8,128)} fusion(f32[2048,128]{1,0:T(8,128)S(1)} %copy-done.1, s32[2048]{0:T(1024)S(1)} %broadcast_clamp_fusion), kind=kCustom, calls=%fused_computation | custom fusion | bytes 2105344 | tf_op jit(solution)/shard_map/gather | solution.py:140
  126.4 2.6 copy.45
  131.5 13.2 %collective-permute-start.7 = (bf16[2048,192]{0,1:T(8,128)(2,1)}, bf16[2048,192]{0,1:T(8,128)(2,1)S(1)}, u32[]{:S(2)}, u32[]{:S(2)}) collective-permute-start(bf16[2048,192]{0,1:T(8,128)(2,1)} %collective-permute-done.6), channel_id=1, source_target_pairs={{1,0},{2,1},{3,2},{4,3},{5,4},{6,5},{7,6},{9,8},{10,9},{11,10},{12... | collective-permute-start | bytes 2359304 | tf_op jit(solution)/shard_map/ppermute | solution.py:12
  144.7 1.9 collective-permute-start.5
  150.0 9.5 %while.51 = (s32[]{:T(128)}, f32[256,128]{1,0:T(8,128)S(1)}, s32[4]{0:T(128)S(1)}, bf16[1,256,64]{2,1,0:T(8,128)(2,1)S(1)}, bf16[4,256,64]{2,1,0:T(8,128)(2,1)},...) while((s32[]{:T(128)}, f32[256,128]{1,0:T(8,128)S(1)}, s32[4]{0:T(128)S(1)}, ...), condition=%wide.region_12.13_spmd, body=%wide.region_7.12_spmd.sunk | while | flops 25624072 | bytes 496837 | solution.py:135
  152.4 2.3 conditional.7
  153.5 1.3 fusion.28
  156.0 2.3 conditional.7
  157.0 1.3 fusion.28
  159.6 2.6 collective-permute-start.8
  162.2 2.2 constant_dynamic-update-slice_fusion.14
  164.3 2.2 constant_dynamic-update-slice_fusion.13
  166.5 2.1 constant_dynamic-update-slice_fusion.12
  169.7 2.1 constant_dynamic-update-slice_fusion.10
  173.9 9.3 %copy.43 = bf16[14336,192]{1,0:T(8,128)(2,1)} copy(bf16[14336,192]{0,1:T(8,128)(2,1)} %constant_dynamic-update-slice_fusion.8) | data formatting | bytes 11010048 | tf_op jit(solution)/shard_map/while | solution.py:83
  184.3 76.1 %while.52 = (s32[]{:T(128)}, f32[2048,128]{1,0:T(8,128)}, s32[]{:T(128)}, s32[8]{0:T(128)S(1)}, bf16[2048,64]{1,0:T(8,128)(2,1)S(1)}, /*index=5*/bf16[14336,192]...) while((s32[]{:T(128)}, f32[2048,128]{1,0:T(8,128)}, ...), condition=%wide.region_18.19_spmd, body=%wide.region_13.18_spmd.sunk | while | flops 1632628736 | bytes 3966781 | solution.py:83
  185.4 9.7 %conditional.8 = (f32[2048,128]{1,0:T(8,128)}) conditional(s32[]{:T(128)} %convert_element_type.117, f32[2048,128]{1,0:T(8,128)} %get-tuple-element.708, (bf16[2048,64]{1,0:T(8,128)(2,1)S(1)}, s32[]{:T(128)}, bf16[14336,192]{1,0:T(8,128)(2,1)}, f32[2048,128]{1,0:T(8,128)}) %tuple.139), branch_computations={%region_14.14_spmd, %region_15.17_spmd} | conditional | flops 1632628736 | bytes 3966534 | solution.py:81
  185.4 1.7 multiply_reduce_fusion.4
  187.1 8.1 %convolution_add_fusion = f32[2048,128]{1,0:T(8,128)} fusion(f32[2048,128]{1,0:T(8,128)} %get-tuple-element.471, bf16[2048,64]{1,0:T(8,128)(2,1)S(1)} %get-tuple-element.472, f32[2048]{0:T(1024)S(1)} %get-tuple-element.582, f32[2048]{0:T(1024)S(1)} %get-tuple-element.583, bf16[14336,192]{1,0:T(8,128)(2,1)} %get-tuple-element.473, s32[]{:T(128)S(6)} %select_n.56, ...), kind=kOutput, calls=%fused_computation.47 | convolution fusion | flops 1631846400 | bytes 3425792 | tf_op jit(solution)/shard_map/while/body/eval_jaxpr/cond/branch_1_fun/dot_general | solution.py:77
  196.3 9.8 %conditional.8 = (f32[2048,128]{1,0:T(8,128)}) conditional(s32[]{:T(128)} %convert_element_type.117, f32[2048,128]{1,0:T(8,128)} %get-tuple-element.708, (bf16[2048,64]{1,0:T(8,128)(2,1)S(1)}, s32[]{:T(128)}, bf16[14336,192]{1,0:T(8,128)(2,1)}, f32[2048,128]{1,0:T(8,128)}) %tuple.139), branch_computations={%region_14.14_spmd, %region_15.17_spmd} | conditional | flops 1632628736 | bytes 3966534 | solution.py:81
  196.3 1.7 multiply_reduce_fusion.4
  197.9 8.1 %convolution_add_fusion = f32[2048,128]{1,0:T(8,128)} fusion(f32[2048,128]{1,0:T(8,128)} %get-tuple-element.471, bf16[2048,64]{1,0:T(8,128)(2,1)S(1)} %get-tuple-element.472, f32[2048]{0:T(1024)S(1)} %get-tuple-element.582, f32[2048]{0:T(1024)S(1)} %get-tuple-element.583, bf16[14336,192]{1,0:T(8,128)(2,1)} %get-tuple-element.473, s32[]{:T(128)S(6)} %select_n.56, ...), kind=kOutput, calls=%fused_computation.47 | convolution fusion | flops 1631846400 | bytes 3425792 | tf_op jit(solution)/shard_map/while/body/eval_jaxpr/cond/branch_1_fun/dot_general | solution.py:77
  207.1 9.7 %conditional.8 = (f32[2048,128]{1,0:T(8,128)}) conditional(s32[]{:T(128)} %convert_element_type.117, f32[2048,128]{1,0:T(8,128)} %get-tuple-element.708, (bf16[2048,64]{1,0:T(8,128)(2,1)S(1)}, s32[]{:T(128)}, bf16[14336,192]{1,0:T(8,128)(2,1)}, f32[2048,128]{1,0:T(8,128)}) %tuple.139), branch_computations={%region_14.14_spmd, %region_15.17_spmd} | conditional | flops 1632628736 | bytes 3966534 | solution.py:81
  207.2 1.7 multiply_reduce_fusion.4
  208.8 8.1 %convolution_add_fusion = f32[2048,128]{1,0:T(8,128)} fusion(f32[2048,128]{1,0:T(8,128)} %get-tuple-element.471, bf16[2048,64]{1,0:T(8,128)(2,1)S(1)} %get-tuple-element.472, f32[2048]{0:T(1024)S(1)} %get-tuple-element.582, f32[2048]{0:T(1024)S(1)} %get-tuple-element.583, bf16[14336,192]{1,0:T(8,128)(2,1)} %get-tuple-element.473, s32[]{:T(128)S(6)} %select_n.56, ...), kind=kOutput, calls=%fused_computation.47 | convolution fusion | flops 1631846400 | bytes 3425792 | tf_op jit(solution)/shard_map/while/body/eval_jaxpr/cond/branch_1_fun/dot_general | solution.py:77
  218.0 9.7 %conditional.8 = (f32[2048,128]{1,0:T(8,128)}) conditional(s32[]{:T(128)} %convert_element_type.117, f32[2048,128]{1,0:T(8,128)} %get-tuple-element.708, (bf16[2048,64]{1,0:T(8,128)(2,1)S(1)}, s32[]{:T(128)}, bf16[14336,192]{1,0:T(8,128)(2,1)}, f32[2048,128]{1,0:T(8,128)}) %tuple.139), branch_computations={%region_14.14_spmd, %region_15.17_spmd} | conditional | flops 1632628736 | bytes 3966534 | solution.py:81
  218.0 1.7 multiply_reduce_fusion.4
  219.7 8.1 %convolution_add_fusion = f32[2048,128]{1,0:T(8,128)} fusion(f32[2048,128]{1,0:T(8,128)} %get-tuple-element.471, bf16[2048,64]{1,0:T(8,128)(2,1)S(1)} %get-tuple-element.472, f32[2048]{0:T(1024)S(1)} %get-tuple-element.582, f32[2048]{0:T(1024)S(1)} %get-tuple-element.583, bf16[14336,192]{1,0:T(8,128)(2,1)} %get-tuple-element.473, s32[]{:T(128)S(6)} %select_n.56, ...), kind=kOutput, calls=%fused_computation.47 | convolution fusion | flops 1631846400 | bytes 3425792 | tf_op jit(solution)/shard_map/while/body/eval_jaxpr/cond/branch_1_fun/dot_general | solution.py:77
  228.9 9.7 %conditional.8 = (f32[2048,128]{1,0:T(8,128)}) conditional(s32[]{:T(128)} %convert_element_type.117, f32[2048,128]{1,0:T(8,128)} %get-tuple-element.708, (bf16[2048,64]{1,0:T(8,128)(2,1)S(1)}, s32[]{:T(128)}, bf16[14336,192]{1,0:T(8,128)(2,1)}, f32[2048,128]{1,0:T(8,128)}) %tuple.139), branch_computations={%region_14.14_spmd, %region_15.17_spmd} | conditional | flops 1632628736 | bytes 3966534 | solution.py:81
  228.9 1.7 multiply_reduce_fusion.4
  230.5 8.1 %convolution_add_fusion = f32[2048,128]{1,0:T(8,128)} fusion(f32[2048,128]{1,0:T(8,128)} %get-tuple-element.471, bf16[2048,64]{1,0:T(8,128)(2,1)S(1)} %get-tuple-element.472, f32[2048]{0:T(1024)S(1)} %get-tuple-element.582, f32[2048]{0:T(1024)S(1)} %get-tuple-element.583, bf16[14336,192]{1,0:T(8,128)(2,1)} %get-tuple-element.473, s32[]{:T(128)S(6)} %select_n.56, ...), kind=kOutput, calls=%fused_computation.47 | convolution fusion | flops 1631846400 | bytes 3425792 | tf_op jit(solution)/shard_map/while/body/eval_jaxpr/cond/branch_1_fun/dot_general | solution.py:77
  239.7 9.7 %conditional.8 = (f32[2048,128]{1,0:T(8,128)}) conditional(s32[]{:T(128)} %convert_element_type.117, f32[2048,128]{1,0:T(8,128)} %get-tuple-element.708, (bf16[2048,64]{1,0:T(8,128)(2,1)S(1)}, s32[]{:T(128)}, bf16[14336,192]{1,0:T(8,128)(2,1)}, f32[2048,128]{1,0:T(8,128)}) %tuple.139), branch_computations={%region_14.14_spmd, %region_15.17_spmd} | conditional | flops 1632628736 | bytes 3966534 | solution.py:81
  239.7 1.7 multiply_reduce_fusion.4
  241.4 8.1 %convolution_add_fusion = f32[2048,128]{1,0:T(8,128)} fusion(f32[2048,128]{1,0:T(8,128)} %get-tuple-element.471, bf16[2048,64]{1,0:T(8,128)(2,1)S(1)} %get-tuple-element.472, f32[2048]{0:T(1024)S(1)} %get-tuple-element.582, f32[2048]{0:T(1024)S(1)} %get-tuple-element.583, bf16[14336,192]{1,0:T(8,128)(2,1)} %get-tuple-element.473, s32[]{:T(128)S(6)} %select_n.56, ...), kind=kOutput, calls=%fused_computation.47 | convolution fusion | flops 1631846400 | bytes 3425792 | tf_op jit(solution)/shard_map/while/body/eval_jaxpr/cond/branch_1_fun/dot_general | solution.py:77
  250.6 9.8 %conditional.8 = (f32[2048,128]{1,0:T(8,128)}) conditional(s32[]{:T(128)} %convert_element_type.117, f32[2048,128]{1,0:T(8,128)} %get-tuple-element.708, (bf16[2048,64]{1,0:T(8,128)(2,1)S(1)}, s32[]{:T(128)}, bf16[14336,192]{1,0:T(8,128)(2,1)}, f32[2048,128]{1,0:T(8,128)}) %tuple.139), branch_computations={%region_14.14_spmd, %region_15.17_spmd} | conditional | flops 1632628736 | bytes 3966534 | solution.py:81
  250.6 1.7 multiply_reduce_fusion.4
  252.3 8.1 %convolution_add_fusion = f32[2048,128]{1,0:T(8,128)} fusion(f32[2048,128]{1,0:T(8,128)} %get-tuple-element.471, bf16[2048,64]{1,0:T(8,128)(2,1)S(1)} %get-tuple-element.472, f32[2048]{0:T(1024)S(1)} %get-tuple-element.582, f32[2048]{0:T(1024)S(1)} %get-tuple-element.583, bf16[14336,192]{1,0:T(8,128)(2,1)} %get-tuple-element.473, s32[]{:T(128)S(6)} %select_n.56, ...), kind=kOutput, calls=%fused_computation.47 | convolution fusion | flops 1631846400 | bytes 3425792 | tf_op jit(solution)/shard_map/while/body/eval_jaxpr/cond/branch_1_fun/dot_general | solution.py:77
  260.4 1.6 copy.44
  262.0 2.9 %fusion.56 = f32[2048,128]{0,1:T(8,128)} fusion(f32[2048,128]{0,1:T(8,128)S(1)} %copy-done.3, f32[2048,128]{0,1:T(8,128)} %copy.45, f32[2048,128]{0,1:T(8,128)S(1)} %copy.44, bf16[2048,256]{1,0:T(8,128)(2,1)S(1)} %copy-done, f32[256,128]{0,1:T(8,128)S(1)} %copy-done.9, f32[128]{0:T(128)S(1)} %copy-done.15, bf16[1,256,256]{2,1,0:T(8,128)(2,1)S(1)} %copy-done.8, ...), kind=kOutput, calls=%fused_computation.58 | convolution fusion | flops 152141824 | bytes 5636608 | tf_op jit(solution)/shard_map/dot_general | solution.py:139
  264.9 2.5 copy.47
  (94 shorter events, 26.7 us)
Async XLA Ops:
  0.0 10.4 %copy-start = (bf16[2048,256]{1,0:T(8,128)(2,1)S(1)}, bf16[2048,256]{1,0:T(8,128)(2,1)}, u32[]{:S(2)}) copy-start(bf16[2048,256]{1,0:T(8,128)(2,1)} %param.29) | copy-start | bytes 3145732
  0.0 84.9 %copy-start.4 = (bf16[2048,64]{0,1:T(8,128)(2,1)S(1)}, bf16[2048,64]{0,1:T(8,128)(2,1)}, u32[]{:S(2)}) copy-start(bf16[2048,64]{0,1:T(8,128)(2,1)} %param.24) | copy-start | bytes 786436
  0.0 10.9 %copy-start.7 = (bf16[1,256,256]{2,1,0:T(8,128)(2,1)S(1)}, bf16[1,256,256]{2,1,0:T(8,128)(2,1)}, u32[]{:S(2)}) copy-start(bf16[1,256,256]{2,1,0:T(8,128)(2,1)} %param.30) | copy-start | bytes 393220
  0.0 38.1 %copy-start.14 = (s32[1,2048]{1,0:T(1,128)S(1)}, s32[1,2048]{1,0:T(1,128)}, u32[]{:S(2)}) copy-start(s32[1,2048]{1,0:T(1,128)} %param.25) | copy-start | bytes 24580
  0.0 67.9 %copy-start.13 = (bf16[1,256,64]{1,2,0:T(8,128)(2,1)S(1)}, bf16[1,256,64]{1,2,0:T(8,128)(2,1)}, u32[]{:S(2)}) copy-start(bf16[1,256,64]{1,2,0:T(8,128)(2,1)} %param.31) | copy-start | bytes 98308
  1.7 1.0 copy-start.2
  2.7 116.0 %copy-start.1 = (f32[2048,128]{1,0:T(8,128)S(1)}, f32[2048,128]{1,0:T(8,128)}, u32[]{:S(2)}) copy-start(f32[2048,128]{1,0:T(8,128)} %param.27) | copy-start | bytes 3145732
  4.8 33.4 %collective-permute-start.3 = (bf16[2048,192]{0,1:T(8,128)(2,1)}, bf16[2048,192]{0,1:T(8,128)(2,1)}, u32[]{:S(2)}, u32[]{:S(2)}) collective-permute-start(bf16[2048,192]{0,1:T(8,128)(2,1)} %pad_maximum_fusion), channel_id=1, source_target_pairs={{0,1},{1,2},{2,3},{3,4},{4,5},{5,6},{6,7},{8,9},{9,10},{10,11},{11... | collective-permute-start | bytes 2359304 | tf_op jit(solution)/shard_map/ppermute | solution.py:12
  8.5 123.0 %collective-permute-start.6 = (bf16[2048,192]{0,1:T(8,128)(2,1)}, bf16[2048,192]{0,1:T(8,128)(2,1)}, u32[]{:S(2)}, u32[]{:S(2)}) collective-permute-start(bf16[2048,192]{0,1:T(8,128)(2,1)} %pad_maximum_fusion), channel_id=1, source_target_pairs={{1,0},{2,1},{3,2},{4,3},{5,4},{6,5},{7,6},{9,8},{10,9},{11,10},{12... | collective-permute-start | bytes 2359304 | tf_op jit(solution)/shard_map/ppermute | solution.py:12
  37.9 47.3 %copy-start.5 = (bf16[256,128]{0,1:T(8,128)(2,1)}, bf16[256,128]{0,1:T(8,128)(2,1)S(1)}, u32[]{:S(2)}) copy-start(bf16[256,128]{0,1:T(8,128)(2,1)S(1)} %all-reduce.1) | copy-start | bytes 196612
  37.9 24.7 %collective-permute-start = (bf16[1,256,128]{1,2,0:T(8,128)(2,1)S(1)}, bf16[1,256,128]{1,2,0:T(8,128)(2,1)S(1)}, u32[]{:S(2)}, u32[]{:S(2)}) collective-permute-start(bf16[1,256,128]{1,2,0:T(8,128)(2,1)S(1)} %bitcast.116), channel_id=1, source_target_pairs={{0,8},{8,16},{16,24},{24,0},{1,9},{9,17},{17,25},{25,1},{2,10},{10... | collective-permute-start | bytes 196616 | tf_op jit(solution)/shard_map/ppermute | solution.py:118
  38.2 106.5 %collective-permute-start.4 = (bf16[2048,192]{0,1:T(8,128)(2,1)}, bf16[2048,192]{0,1:T(8,128)(2,1)}, u32[]{:S(2)}, u32[]{:S(2)}) collective-permute-start(bf16[2048,192]{0,1:T(8,128)(2,1)} %collective-permute-done.3), channel_id=1, source_target_pairs={{0,1},{1,2},{2,3},{3,4},{4,5},{5,6},{6,7},{8,9},{9,10},{10,11},{11... | collective-permute-start | bytes 2359304 | tf_op jit(solution)/shard_map/ppermute | solution.py:12
  62.6 22.3 %copy-start.12 = (bf16[1,256,128]{1,2,0:T(8,128)(2,1)}, bf16[1,256,128]{1,2,0:T(8,128)(2,1)S(1)}, u32[]{:S(2)}) copy-start(bf16[1,256,128]{1,2,0:T(8,128)(2,1)S(1)} %collective-permute-done) | copy-start | bytes 196612
  62.6 3.2 %collective-permute-start.1 = (bf16[1,256,128]{1,2,0:T(8,128)(2,1)S(1)}, bf16[1,256,128]{1,2,0:T(8,128)(2,1)}, u32[]{:S(2)}, u32[]{:S(2)}) collective-permute-start(bf16[1,256,128]{1,2,0:T(8,128)(2,1)S(1)} %collective-permute-done), channel_id=1, source_target_pairs={{0,8},{8,16},{16,24},{24,0},{1,9},{9,17},{17,25},{25,1},{2,10},{10... | collective-permute-start | bytes 196616 | tf_op jit(solution)/shard_map/ppermute | solution.py:118
  65.8 63.1 %collective-permute-start.2 = (bf16[1,256,128]{1,2,0:T(8,128)(2,1)}, bf16[1,256,128]{1,2,0:T(8,128)(2,1)}, u32[]{:S(2)}, u32[]{:S(2)}) collective-permute-start(bf16[1,256,128]{1,2,0:T(8,128)(2,1)} %collective-permute-done.1), channel_id=1, source_target_pairs={{0,8},{8,16},{16,24},{24,0},{1,9},{9,17},{17,25},{25,1},{2,10},{10... | collective-permute-start | bytes 196616 | tf_op jit(solution)/shard_map/ppermute | solution.py:118
  118.8 27.8 %copy-start.6 = (bf16[256,128]{0,1:T(8,128)(2,1)S(1)}, bf16[256,128]{0,1:T(8,128)(2,1)}, u32[]{:S(2)}) copy-start(bf16[256,128]{0,1:T(8,128)(2,1)} %copy-done.5) | copy-start | bytes 196612
  118.8 31.3 %copy-start.16 = (s32[1,4]{1,0:T(1,128)S(1)}, s32[1,4]{1,0:T(1,128)}, u32[]{:S(2)}) copy-start(s32[1,4]{1,0:T(1,128)} %param.35) | copy-start | bytes 52
  131.5 28.1 %collective-permute-start.7 = (bf16[2048,192]{0,1:T(8,128)(2,1)}, bf16[2048,192]{0,1:T(8,128)(2,1)S(1)}, u32[]{:S(2)}, u32[]{:S(2)}) collective-permute-start(bf16[2048,192]{0,1:T(8,128)(2,1)} %collective-permute-done.6), channel_id=1, source_target_pairs={{1,0},{2,1},{3,2},{4,3},{5,4},{6,5},{7,6},{9,8},{10,9},{11,10},{12... | collective-permute-start | bytes 2359304 | tf_op jit(solution)/shard_map/ppermute | solution.py:12
  144.7 17.5 %collective-permute-start.5 = (bf16[2048,192]{0,1:T(8,128)(2,1)}, bf16[2048,192]{0,1:T(8,128)(2,1)}, u32[]{:S(2)}, u32[]{:S(2)}) collective-permute-start(bf16[2048,192]{0,1:T(8,128)(2,1)} %collective-permute-done.4), channel_id=1, source_target_pairs={{0,1},{1,2},{2,3},{3,4},{4,5},{5,6},{6,7},{8,9},{9,10},{10,11},{11... | collective-permute-start | bytes 2359304 | tf_op jit(solution)/shard_map/ppermute | solution.py:12
  159.5 14.3 %copy-start.10 = (f32[256,128]{1,0:T(8,128)}, f32[256,128]{1,0:T(8,128)S(1)}, u32[]{:S(2)}) copy-start(f32[256,128]{1,0:T(8,128)S(1)} %get-tuple-element.486) | copy-start | bytes 393220
  159.6 13.3 %collective-permute-start.8 = (bf16[2048,192]{0,1:T(8,128)(2,1)S(1)}, bf16[2048,192]{0,1:T(8,128)(2,1)S(1)}, u32[]{:S(2)}, u32[]{:S(2)}) collective-permute-start(bf16[2048,192]{0,1:T(8,128)(2,1)S(1)} %collective-permute-done.7), channel_id=1, source_target_pairs={{1,0},{2,1},{3,2},{4,3},{5,4},{6,5},{7,6},{9,8},{10,9},{11,10},{12... | collective-permute-start | bytes 2359304 | tf_op jit(solution)/shard_map/ppermute | solution.py:12
  173.9 10.4 %copy-start.17 = (s32[1,8]{1,0:T(1,128)S(1)}, s32[1,8]{1,0:T(1,128)}, u32[]{:S(2)}) copy-start(s32[1,8]{1,0:T(1,128)} %param.33) | copy-start | bytes 100
  184.2 77.7 %copy-start.3 = (f32[2048,128]{0,1:T(8,128)S(1)}, f32[2048,128]{0,1:T(8,128)}, u32[]{:S(2)}) copy-start(f32[2048,128]{0,1:T(8,128)} %copy-done.2) | copy-start | bytes 3145732
  184.2 77.7 %copy-start.8 = (bf16[1,256,256]{2,1,0:T(8,128)(2,1)S(1)}, bf16[1,256,256]{2,1,0:T(8,128)(2,1)}, u32[]{:S(2)}) copy-start(bf16[1,256,256]{2,1,0:T(8,128)(2,1)} %param.30) | copy-start | bytes 393220
  184.2 77.7 %copy-start.9 = (f32[256,128]{0,1:T(8,128)S(1)}, f32[256,128]{0,1:T(8,128)}, u32[]{:S(2)}) copy-start(f32[256,128]{0,1:T(8,128)} %copy.41) | copy-start | bytes 393220
  184.2 77.7 %copy-start.11 = (f32[256,128]{1,0:T(8,128)S(1)}, f32[256,128]{1,0:T(8,128)}, u32[]{:S(2)}) copy-start(f32[256,128]{1,0:T(8,128)} %copy-done.10) | copy-start | bytes 393220
  184.2 77.7 %copy-start.15 = (f32[128]{0:T(128)S(1)}, f32[128]{0:T(128)}, u32[]{:S(2)}) copy-start(f32[128]{0:T(128)} %param.28) | copy-start | bytes 1540
